TPU v7x, 32 devices: a whole 2x2x4 slice. The times are simulated.
32 devices in a mesh: site: 4 (over y, x), sector: 8 (over z, core).
Axes of the slice: x: 2, y: 2, z: 4, core: 2. Of those that a mesh axis runs over, the one named last changes fastest.
Arguments:
- boundary: bfloat16 [4, 2048, 32, 256], P('site', 'sector'), may hold values from -0.375 to 0.375
- peps_row: bfloat16 [4, 32, 8], P('site'), may hold values from -1 to 1
- sketch: bfloat16 [4, 2048, 8, 256], P('site', 'sector'), may hold values from -0.125 to 0.125
- charges: int32 [4, 8], P('site'), may hold values from -1 to 1
- left_edge: bfloat16 [512, 2048], P(None, 'sector'), may hold values from -6 to 6
Outputs:
- environments: float32 [4, 512, 2048], P('site', None, 'sector')
Inputs may be any that keep to these rules, and one draw needn't show every extreme that they name: `charges`: each entry is a charge change of -1, 0 or +1.
All inputs are finite; a program needn't handle non-finite values.
Results may differ from a plain program's by a relative error of at most 0.0003.
Values sent between devices are 32-bit elements; how exact they have to be, the bound alone decides.
A program may use at most 64 MiB of HBM per device.

v0:
```python
import jax
import jax.numpy as jnp
from jax import lax
from jax.sharding import PartitionSpec as P


def with_halo(block, sides, width):
    for axis, dim in sides:
        count = lax.axis_size(axis)
        forward = [(i, i + 1) for i in range(count - 1)]
        backward = [(target, source) for source, target in forward]
        low = lax.ppermute(
            lax.slice_in_dim(block, block.shape[dim] - width, None, axis=dim), axis, forward
        )
        high = lax.ppermute(lax.slice_in_dim(block, 0, width, axis=dim), axis, backward)
        block = jnp.concatenate([low, block, high], axis=dim)
    return block


def local(boundary, peps_row, sketch, charges, left_edge):
    total_rows = left_edge.shape[0]
    absorbed = jnp.einsum("jwpv,jpl->jwlv", boundary, peps_row, preferred_element_type=jnp.float32)
    sketch_wide = sketch.astype(jnp.float32)
    onehot = (charges[:, :, None] == jnp.arange(-1, 2, dtype=jnp.int32)[None, None, :]).astype(
        jnp.float32
    )
    site_devices = lax.axis_size("site")
    position = lax.axis_index("site")
    own_maps = jnp.einsum(
        "jwlv,jvlu,jls->jswu", absorbed, sketch_wide, onehot, precision=lax.Precision.HIGHEST
    )
    all_maps = lax.all_gather(own_maps, "site", axis=0, tiled=True)
    share_rows = total_rows // site_devices
    start_state = lax.dynamic_slice_in_dim(left_edge, position * share_rows, share_rows, 0).astype(
        jnp.float32
    )

    def row_site(state_rows, site_map):
        parts = jnp.einsum("rw,swu->sru", state_rows, site_map, precision=lax.Precision.HIGHEST)
        outflow = jnp.stack([parts[0], parts[2]], axis=0)
        padded = with_halo(outflow, (("sector", 0),), 1)
        updated = parts[1] + padded[0] + padded[3]
        return (updated, updated)

    final_rows, stacked = lax.scan(row_site, start_state, all_maps)
    return lax.all_to_all(stacked, "site", split_axis=0, concat_axis=1, tiled=True)


def solution(mesh):
    in_specs = (
        P("site", "sector", None, None),
        P("site", None, None),
        P("site", "sector", None, None),
        P("site", None),
        P(None, "sector"),
    )
    out_specs = P("site", None, "sector")
    return jax.shard_map(local, mesh=mesh, in_specs=in_specs, out_specs=out_specs, check_vma=False)
```

profile of v0, /device:TPU:8, one launch (start us, length us, event | category | flops | bytes accessed | tf_op | source)
XLA Modules:
  0.0 126.1 jit_solution(7024198187606349648)
XLA Ops:
  6.5 2.9 %fusion.12 = f32[256,8,256]{2,1,0:T(8,128)S(1)} fusion(bf16[1,256,32,256]{3,2,1,0:T(8,128)(2,1)} %param.7, bf16[1,32,8]{1,2,0:T(8,128)(2,1)} %param.8), kind=kOutput, calls=%fused_computation.15 | convolution fusion | flops 33554432 | bytes 6291968 | tf_op jit(solution)/shard_map/jwpv,jpl->jwlv/dot_general | solution.py:22
  9.5 3.1 %fusion.10 = f32[8,256,256]{2,1,0:T(8,128)} fusion(f32[256,8,256]{2,1,0:T(8,128)S(1)} %fusion.12, bf16[256,8,256]{2,1,0:T(8,128)(2,1)S(1)} %bitcast.47), kind=kOutput, calls=%fused_computation.13 | convolution fusion | flops 1610612736 | bytes 5242880 | tf_op jit(solution)/shard_map/jwlv,jvlu,jls->jswu/dot_general | solution.py:29
  12.6 2.2 %copy.18 = f32[8,256,256]{1,0,2:T(8,128)S(1)} copy(f32[8,256,256]{2,1,0:T(8,128)} %fusion.10) | data formatting | bytes 4194304 | tf_op jit(solution)/shard_map/jwlv,jvlu,jls->jswu/dot_general | solution.py:29
  14.8 2.1 %fusion.15 = f32[1,3,256,256]{2,1,3,0:T(4,128)} fusion(f32[8,256,256]{1,0,2:T(8,128)S(1)} %copy.18, s32[8]{0:T(128)S(1)} %bitcast.48, s32[3]{0:T(128)S(1)} %iota_add_fusion), kind=kOutput, calls=%fused_computation.16 | convolution fusion | flops 18874392 | bytes 2883628 | tf_op jit(solution)/shard_map/jwlv,jvlu,jls->jswu/dot_general | solution.py:29
  16.9 2.4 %copy.12 = f32[1,3,256,256]{3,2,1,0:T(8,128)} copy(f32[1,3,256,256]{2,1,3,0:T(4,128)} %fusion.15) | data formatting | bytes 1572864 | tf_op jit(solution)/shard_map/jwlv,jvlu,jls->jswu/transpose | solution.py:29
  19.3 0.0 all-gather.2.cloned.1.call-update
  19.3 0.8 constant_dynamic-slice_fusion
  20.2 0.1 copy.21
  20.3 44.2 %all-gather.2.cloned.1.call-done = f32[4,3,256,256]{3,2,1,0:T(8,128)} async-done(((f32[1,3,256,256]{3,2,1,0:T(8,128)}), f32[4,3,256,256]{3,2,1,0:T(8,128)}) %all-gather.2.cloned.1.call-update) | async-done | bytes 3145744 | tf_op jit(solution)/shard_map/all_gather | solution.py:32
  64.5 43.3 %while.12 = (s32[]{:T(128)}, f32[128,256]{0,1:T(8,128)S(1)}, f32[4,128,256]{1,2,0:T(8,128)S(1)}, f32[4,3,256,256]{3,2,1,0:T(8,128)}, s32[]{:T(128)}) while((s32[]{:T(128)}, f32[128,256]{0,1:T(8,128)S(1)}, f32[4,128,256]{1,2,0:T(8,128)S(1)}, f32[4,3,256,256]{3,2,1,0:T(8,128)}, s32[]{:T(128)}) %tuple.26), condition=%wide.region_1.2_spmd, body=%wide.region_0.1_spmd.sunk | while | flops 302055424 | bytes 3539101 | solution.py:45
  64.5 2.5 %convolution_bitcast_fusion.2 = f32[3,128,256]{1,2,0:T(8,128)S(1)} fusion(f32[4,3,256,256]{3,2,1,0:T(8,128)} %get-tuple-element.94, s32[]{:T(128)S(6)} %copy.30, f32[128,256]{0,1:T(8,128)S(1)} %get-tuple-element.87), kind=kOutput, calls=%fused_computation.clone.1 | convolution fusion | flops 301989888 | bytes 1310724 | tf_op jit(solution)/shard_map/while/body/eval_jaxpr/rw,swu->sru/dot_general | solution.py:39
  67.0 1.9 %collective-permute-start = (f32[1,128,256]{1,2,0:T(8,128)S(1)}, f32[1,128,256]{1,2,0:T(8,128)S(1)}, u32[]{:S(2)}, u32[]{:S(2)}) collective-permute-start(f32[1,128,256]{1,2,0:T(8,128)S(1)} %get-tuple-element.77), channel_id=1, source_target_pairs={{1,0},{2,1},{3,2},{4,3},{5,4},{6,5},{7,6},{9,8},{10,9},{11,10},{12... | collective-permute-start | bytes 393224 | tf_op jit(solution)/shard_map/while/body/eval_jaxpr/ppermute | solution.py:15
  69.0 2.4 %collective-permute-start.1 = (f32[1,128,256]{1,2,0:T(8,128)S(1)}, f32[1,128,256]{1,2,0:T(8,128)S(1)}, u32[]{:S(2)}, u32[]{:S(2)}) collective-permute-start(f32[1,128,256]{1,2,0:T(8,128)S(1)} %get-tuple-element.78), channel_id=1, source_target_pairs={{0,1},{1,2},{2,3},{3,4},{4,5},{5,6},{6,7},{8,9},{9,10},{10,11},{11... | collective-permute-start | bytes 393224 | tf_op jit(solution)/shard_map/while/body/eval_jaxpr/ppermute | solution.py:12
  71.4 0.1 collective-permute-done
  71.5 3.8 %collective-permute-done.1 = f32[1,128,256]{1,2,0:T(8,128)S(1)} collective-permute-done((f32[1,128,256]{1,2,0:T(8,128)S(1)}, f32[1,128,256]{1,2,0:T(8,128)S(1)}, u32[]{:S(2)}, u32[]{:S(2)}) %collective-permute-start.1) | collective-permute-done | bytes 131104 | tf_op jit(solution)/shard_map/while/body/eval_jaxpr/ppermute | solution.py:12
  75.3 2.5 %convolution_bitcast_fusion.2 = f32[3,128,256]{1,2,0:T(8,128)S(1)} fusion(f32[4,3,256,256]{3,2,1,0:T(8,128)} %get-tuple-element.94, s32[]{:T(128)S(6)} %copy.30, f32[128,256]{0,1:T(8,128)S(1)} %get-tuple-element.87), kind=kOutput, calls=%fused_computation.clone.1 | convolution fusion | flops 301989888 | bytes 1310724 | tf_op jit(solution)/shard_map/while/body/eval_jaxpr/rw,swu->sru/dot_general | solution.py:39
  77.9 1.9 %collective-permute-start = (f32[1,128,256]{1,2,0:T(8,128)S(1)}, f32[1,128,256]{1,2,0:T(8,128)S(1)}, u32[]{:S(2)}, u32[]{:S(2)}) collective-permute-start(f32[1,128,256]{1,2,0:T(8,128)S(1)} %get-tuple-element.77), channel_id=1, source_target_pairs={{1,0},{2,1},{3,2},{4,3},{5,4},{6,5},{7,6},{9,8},{10,9},{11,10},{12... | collective-permute-start | bytes 393224 | tf_op jit(solution)/shard_map/while/body/eval_jaxpr/ppermute | solution.py:15
  79.8 2.4 %collective-permute-start.1 = (f32[1,128,256]{1,2,0:T(8,128)S(1)}, f32[1,128,256]{1,2,0:T(8,128)S(1)}, u32[]{:S(2)}, u32[]{:S(2)}) collective-permute-start(f32[1,128,256]{1,2,0:T(8,128)S(1)} %get-tuple-element.78), channel_id=1, source_target_pairs={{0,1},{1,2},{2,3},{3,4},{4,5},{5,6},{6,7},{8,9},{9,10},{10,11},{11... | collective-permute-start | bytes 393224 | tf_op jit(solution)/shard_map/while/body/eval_jaxpr/ppermute | solution.py:12
  82.2 0.1 collective-permute-done
  82.3 3.8 %collective-permute-done.1 = f32[1,128,256]{1,2,0:T(8,128)S(1)} collective-permute-done((f32[1,128,256]{1,2,0:T(8,128)S(1)}, f32[1,128,256]{1,2,0:T(8,128)S(1)}, u32[]{:S(2)}, u32[]{:S(2)}) %collective-permute-start.1) | collective-permute-done | bytes 131104 | tf_op jit(solution)/shard_map/while/body/eval_jaxpr/ppermute | solution.py:12
  86.1 2.5 %convolution_bitcast_fusion.2 = f32[3,128,256]{1,2,0:T(8,128)S(1)} fusion(f32[4,3,256,256]{3,2,1,0:T(8,128)} %get-tuple-element.94, s32[]{:T(128)S(6)} %copy.30, f32[128,256]{0,1:T(8,128)S(1)} %get-tuple-element.87), kind=kOutput, calls=%fused_computation.clone.1 | convolution fusion | flops 301989888 | bytes 1310724 | tf_op jit(solution)/shard_map/while/body/eval_jaxpr/rw,swu->sru/dot_general | solution.py:39
  88.7 1.9 %collective-permute-start = (f32[1,128,256]{1,2,0:T(8,128)S(1)}, f32[1,128,256]{1,2,0:T(8,128)S(1)}, u32[]{:S(2)}, u32[]{:S(2)}) collective-permute-start(f32[1,128,256]{1,2,0:T(8,128)S(1)} %get-tuple-element.77), channel_id=1, source_target_pairs={{1,0},{2,1},{3,2},{4,3},{5,4},{6,5},{7,6},{9,8},{10,9},{11,10},{12... | collective-permute-start | bytes 393224 | tf_op jit(solution)/shard_map/while/body/eval_jaxpr/ppermute | solution.py:15
  90.6 2.4 %collective-permute-start.1 = (f32[1,128,256]{1,2,0:T(8,128)S(1)}, f32[1,128,256]{1,2,0:T(8,128)S(1)}, u32[]{:S(2)}, u32[]{:S(2)}) collective-permute-start(f32[1,128,256]{1,2,0:T(8,128)S(1)} %get-tuple-element.78), channel_id=1, source_target_pairs={{0,1},{1,2},{2,3},{3,4},{4,5},{5,6},{6,7},{8,9},{9,10},{10,11},{11... | collective-permute-start | bytes 393224 | tf_op jit(solution)/shard_map/while/body/eval_jaxpr/ppermute | solution.py:12
  93.0 0.1 collective-permute-done
  93.1 3.8 %collective-permute-done.1 = f32[1,128,256]{1,2,0:T(8,128)S(1)} collective-permute-done((f32[1,128,256]{1,2,0:T(8,128)S(1)}, f32[1,128,256]{1,2,0:T(8,128)S(1)}, u32[]{:S(2)}, u32[]{:S(2)}) %collective-permute-start.1) | collective-permute-done | bytes 131104 | tf_op jit(solution)/shard_map/while/body/eval_jaxpr/ppermute | solution.py:12
  96.9 2.5 %convolution_bitcast_fusion.2 = f32[3,128,256]{1,2,0:T(8,128)S(1)} fusion(f32[4,3,256,256]{3,2,1,0:T(8,128)} %get-tuple-element.94, s32[]{:T(128)S(6)} %copy.30, f32[128,256]{0,1:T(8,128)S(1)} %get-tuple-element.87), kind=kOutput, calls=%fused_computation.clone.1 | convolution fusion | flops 301989888 | bytes 1310724 | tf_op jit(solution)/shard_map/while/body/eval_jaxpr/rw,swu->sru/dot_general | solution.py:39
  99.5 1.9 %collective-permute-start = (f32[1,128,256]{1,2,0:T(8,128)S(1)}, f32[1,128,256]{1,2,0:T(8,128)S(1)}, u32[]{:S(2)}, u32[]{:S(2)}) collective-permute-start(f32[1,128,256]{1,2,0:T(8,128)S(1)} %get-tuple-element.77), channel_id=1, source_target_pairs={{1,0},{2,1},{3,2},{4,3},{5,4},{6,5},{7,6},{9,8},{10,9},{11,10},{12... | collective-permute-start | bytes 393224 | tf_op jit(solution)/shard_map/while/body/eval_jaxpr/ppermute | solution.py:15
  101.4 2.4 %collective-permute-start.1 = (f32[1,128,256]{1,2,0:T(8,128)S(1)}, f32[1,128,256]{1,2,0:T(8,128)S(1)}, u32[]{:S(2)}, u32[]{:S(2)}) collective-permute-start(f32[1,128,256]{1,2,0:T(8,128)S(1)} %get-tuple-element.78), channel_id=1, source_target_pairs={{0,1},{1,2},{2,3},{3,4},{4,5},{5,6},{6,7},{8,9},{9,10},{10,11},{11... | collective-permute-start | bytes 393224 | tf_op jit(solution)/shard_map/while/body/eval_jaxpr/ppermute | solution.py:12
  103.9 0.1 collective-permute-done
  103.9 3.8 %collective-permute-done.1 = f32[1,128,256]{1,2,0:T(8,128)S(1)} collective-permute-done((f32[1,128,256]{1,2,0:T(8,128)S(1)}, f32[1,128,256]{1,2,0:T(8,128)S(1)}, u32[]{:S(2)}, u32[]{:S(2)}) %collective-permute-start.1) | collective-permute-done | bytes 131104 | tf_op jit(solution)/shard_map/while/body/eval_jaxpr/ppermute | solution.py:12
  107.8 10.5 %all_to_all.12 = f32[4,128,256]{1,2,0:T(8,128)S(1)} all-to-all(f32[4,128,256]{1,2,0:T(8,128)S(1)} %get-tuple-element.27), channel_id=1, replica_groups=mesh['site'=4,'sector'=8] {'site'}, dimensions={0} | all-to-all | bytes 1048576 | tf_op jit(solution)/shard_map/all_to_all | solution.py:46
  118.3 1.0 copy.14
  (16 shorter events, 0.2 us)
Async XLA Ops:
  6.5 3.0 %copy-start = (bf16[1,256,8,256]{3,2,1,0:T(8,128)(2,1)S(1)}, bf16[1,256,8,256]{3,2,1,0:T(8,128)(2,1)}, u32[]{:S(2)}) copy-start(bf16[1,256,8,256]{3,2,1,0:T(8,128)(2,1)} %param.9) | copy-start | bytes 3145732
  6.5 57.9 %all-gather.2.cloned.1.call-start = ((), (), s32[]{:S(2)}) async-start(), calls=%async_computation.1 | async-start | bytes 3932160 | tf_op jit(solution)/shard_map/all_gather | solution.py:32
  12.6 2.2 %copy-start.1 = (s32[1,8]{1,0:T(1,128)S(1)}, s32[1,8]{1,0:T(1,128)}, u32[]{:S(2)}) copy-start(s32[1,8]{1,0:T(1,128)} %param.10) | copy-start | bytes 100
  67.0 4.4 %collective-permute-start = (f32[1,128,256]{1,2,0:T(8,128)S(1)}, f32[1,128,256]{1,2,0:T(8,128)S(1)}, u32[]{:S(2)}, u32[]{:S(2)}) collective-permute-start(f32[1,128,256]{1,2,0:T(8,128)S(1)} %get-tuple-element.77), channel_id=1, source_target_pairs={{1,0},{2,1},{3,2},{4,3},{5,4},{6,5},{7,6},{9,8},{10,9},{11,10},{12... | collective-permute-start | bytes 393224 | tf_op jit(solution)/shard_map/while/body/eval_jaxpr/ppermute | solution.py:15
  69.0 6.3 %collective-permute-start.1 = (f32[1,128,256]{1,2,0:T(8,128)S(1)}, f32[1,128,256]{1,2,0:T(8,128)S(1)}, u32[]{:S(2)}, u32[]{:S(2)}) collective-permute-start(f32[1,128,256]{1,2,0:T(8,128)S(1)} %get-tuple-element.78), channel_id=1, source_target_pairs={{0,1},{1,2},{2,3},{3,4},{4,5},{5,6},{6,7},{8,9},{9,10},{10,11},{11... | collective-permute-start | bytes 393224 | tf_op jit(solution)/shard_map/while/body/eval_jaxpr/ppermute | solution.py:12
  77.9 4.4 %collective-permute-start = (f32[1,128,256]{1,2,0:T(8,128)S(1)}, f32[1,128,256]{1,2,0:T(8,128)S(1)}, u32[]{:S(2)}, u32[]{:S(2)}) collective-permute-start(f32[1,128,256]{1,2,0:T(8,128)S(1)} %get-tuple-element.77), channel_id=1, source_target_pairs={{1,0},{2,1},{3,2},{4,3},{5,4},{6,5},{7,6},{9,8},{10,9},{11,10},{12... | collective-permute-start | bytes 393224 | tf_op jit(solution)/shard_map/while/body/eval_jaxpr/ppermute | solution.py:15
  79.8 6.3 %collective-permute-start.1 = (f32[1,128,256]{1,2,0:T(8,128)S(1)}, f32[1,128,256]{1,2,0:T(8,128)S(1)}, u32[]{:S(2)}, u32[]{:S(2)}) collective-permute-start(f32[1,128,256]{1,2,0:T(8,128)S(1)} %get-tuple-element.78), channel_id=1, source_target_pairs={{0,1},{1,2},{2,3},{3,4},{4,5},{5,6},{6,7},{8,9},{9,10},{10,11},{11... | collective-permute-start | bytes 393224 | tf_op jit(solution)/shard_map/while/body/eval_jaxpr/ppermute | solution.py:12
  88.7 4.4 %collective-permute-start = (f32[1,128,256]{1,2,0:T(8,128)S(1)}, f32[1,128,256]{1,2,0:T(8,128)S(1)}, u32[]{:S(2)}, u32[]{:S(2)}) collective-permute-start(f32[1,128,256]{1,2,0:T(8,128)S(1)} %get-tuple-element.77), channel_id=1, source_target_pairs={{1,0},{2,1},{3,2},{4,3},{5,4},{6,5},{7,6},{9,8},{10,9},{11,10},{12... | collective-permute-start | bytes 393224 | tf_op jit(solution)/shard_map/while/body/eval_jaxpr/ppermute | solution.py:15
  90.6 6.3 %collective-permute-start.1 = (f32[1,128,256]{1,2,0:T(8,128)S(1)}, f32[1,128,256]{1,2,0:T(8,128)S(1)}, u32[]{:S(2)}, u32[]{:S(2)}) collective-permute-start(f32[1,128,256]{1,2,0:T(8,128)S(1)} %get-tuple-element.78), channel_id=1, source_target_pairs={{0,1},{1,2},{2,3},{3,4},{4,5},{5,6},{6,7},{8,9},{9,10},{10,11},{11... | collective-permute-start | bytes 393224 | tf_op jit(solution)/shard_map/while/body/eval_jaxpr/ppermute | solution.py:12
  99.5 4.4 %collective-permute-start = (f32[1,128,256]{1,2,0:T(8,128)S(1)}, f32[1,128,256]{1,2,0:T(8,128)S(1)}, u32[]{:S(2)}, u32[]{:S(2)}) collective-permute-start(f32[1,128,256]{1,2,0:T(8,128)S(1)} %get-tuple-element.77), channel_id=1, source_target_pairs={{1,0},{2,1},{3,2},{4,3},{5,4},{6,5},{7,6},{9,8},{10,9},{11,10},{12... | collective-permute-start | bytes 393224 | tf_op jit(solution)/shard_map/while/body/eval_jaxpr/ppermute | solution.py:15
  101.4 6.3 %collective-permute-start.1 = (f32[1,128,256]{1,2,0:T(8,128)S(1)}, f32[1,128,256]{1,2,0:T(8,128)S(1)}, u32[]{:S(2)}, u32[]{:S(2)}) collective-permute-start(f32[1,128,256]{1,2,0:T(8,128)S(1)} %get-tuple-element.78), channel_id=1, source_target_pairs={{0,1},{1,2},{2,3},{3,4},{4,5},{5,6},{6,7},{8,9},{9,10},{10,11},{11... | collective-permute-start | bytes 393224 | tf_op jit(solution)/shard_map/while/body/eval_jaxpr/ppermute | solution.py:12
Sparse Core Ops, SparseCore 0:
  19.4 44.9 all-gather.1
where the time goes:
time: 127 us; the launch traced here: 126 us
  waiting for transfers between devices  59.7 us (47%)
  matrix products  18.2 us (14%)
  starting transfers between devices  17.3 us (14%)
  between operations  13.5 us (11%)
  blocking collectives  10.5 us (8%)
  local copies, waits for them, and re-layouts  6.64 us (5%)
    all_gather x1, waiting for transfers between devices, local(): all_maps = lax.all_gather(own_maps, 'site', axis=0, tiled=True)  44.2 us
    ppermute x4, waiting for transfers between devices, with_halo(): lax.ppermute(lax.slice_in_dim(block, block.shape[dim] - width, None, axis...  15.1 us
    all_to_all x1, blocking collectives, local(): lax.all_to_all(stacked, 'site', split_axis=0, concat_axis=1, tiled=True)  10.5 us
    dot_general x4, matrix products, row_site(): jnp.einsum('rw,swu->sru', state_rows, site_map, precision=lax.Precision.H...  10.1 us
    ppermute x4, starting transfers between devices, with_halo(): lax.ppermute(lax.slice_in_dim(block, block.shape[dim] - width, None, axis...  9.63 us
    ppermute x4, starting transfers between devices, with_halo(): lax.ppermute(lax.slice_in_dim(block, 0, width, axis=dim), axis, backward)  7.68 us
    dot_general x2, matrix products, local(): jnp.einsum('jwlv,jvlu,jls->jswu', absorbed, sketch_wide, onehot, precisio...  5.17 us
    dot_general x1, matrix products, local(): jnp.einsum('jwpv,jpl->jwlv', boundary, peps_row, preferred_element_type=j...  2.94 us
  transfers between devices with their start and end apart: 9, of which 9 were waited for; matrix products, arithmetic and copies ran while one was open for 1% of the time, Pallas kernels for 0%

commit v1 on v0

--- a/solution.py
+++ b/solution.py
@@ -29,7 +29,12 @@
     own_maps = jnp.einsum(
         "jwlv,jvlu,jls->jswu", absorbed, sketch_wide, onehot, precision=lax.Precision.HIGHEST
     )
-    all_maps = lax.all_gather(own_maps, "site", axis=0, tiled=True)
+    ring = [own_maps]
+    for hop in range(3):
+        ring.append(lax.ppermute(ring[-1], "site", [(dev, (dev + 1) % 4) for dev in range(4)]))
+    all_maps = jnp.roll(
+        jnp.concatenate(ring[::-1], axis=0), (lax.axis_index("site") + 1) * ring[0].shape[0], axis=0
+    )
     share_rows = total_rows // site_devices
     start_state = lax.dynamic_slice_in_dim(left_edge, position * share_rows, share_rows, 0).astype(
         jnp.float32

time: 127 us -> 132 us (1.039)
  between operations: 13.5 us -> 0.16 us
  local copies, waits for them, and re-layouts: 6.64 us -> 19.2 us
  waiting for transfers between devices: 59.7 us -> 66.8 us
  matrix products: 18.2 us -> 15 us
  starting transfers between devices: 17.3 us -> 19.4 us
    ppermute x0 -> x3, waiting for transfers between devices: none -> 51.3 us  [local(): lax.ppermute(ring[-1], 'site', [(dev, (dev + 1) % 4) for dev in range(4)])]
    all_gather x1 -> x0, waiting for transfers between devices: 44.2 us -> none  [local(): all_maps = lax.all_gather(own_maps, 'site', axis=0, tiled=True)]
    ppermute x0 -> x3, local copies, waits for them, and re-layouts: none -> 6.44 us  [local(): lax.ppermute(ring[-1], 'site', [(dev, (dev + 1) % 4) for dev in range(4)])]
    unnamed x5 -> x20, local copies, waits for them, and re-layouts: 0.12 us -> 5.3 us
    dot_general x4, matrix products: 10.1 us -> 7.66 us  [row_site(): jnp.einsum('rw,swu->sru', state_rows, site_map, precision=lax.Precision.H...]
    while x0 -> x1, local copies, waits for them, and re-layouts: none -> 2.19 us  [local(): final_rows, stacked = lax.scan(row_site, start_state, all_maps)]
    ppermute x0 -> x3, starting transfers between devices: none -> 2.14 us  [local(): lax.ppermute(ring[-1], 'site', [(dev, (dev + 1) % 4) for dev in range(4)])]
    transpose x1, local copies, waits for them, and re-layouts: 2.38 us -> 0.32 us  [local(): jnp.einsum('jwlv,jvlu,jls->jswu', absorbed, sketch_wide, onehot, precisio...]
  transfers between devices with their start and end apart: 9 -> 11, of which waited for: 9 -> 11; matrix products, arithmetic and copies ran while one was open for 1% -> 4% of each run, Pallas kernels for 0% -> 0%
where the time goes in v1:
time: 132 us
  waiting for transfers between devices  66.8 us (51%)
  starting transfers between devices  19.4 us (15%)
  local copies, waits for them, and re-layouts  19.2 us (15%)
  matrix products  15 us (11%)
  blocking collectives  10.6 us (8%)
    ppermute x3, waiting for transfers between devices, local(): lax.ppermute(ring[-1], 'site', [(dev, (dev + 1) % 4) for dev in range(4)])  51.3 us
    ppermute x4, waiting for transfers between devices, with_halo(): lax.ppermute(lax.slice_in_dim(block, block.shape[dim] - width, None, axis...  15.1 us
    all_to_all x1, blocking collectives, local(): lax.all_to_all(stacked, 'site', split_axis=0, concat_axis=1, tiled=True)  10.6 us
    ppermute x4, starting transfers between devices, with_halo(): lax.ppermute(lax.slice_in_dim(block, block.shape[dim] - width, None, axis...  9.63 us
    ppermute x4, starting transfers between devices, with_halo(): lax.ppermute(lax.slice_in_dim(block, 0, width, axis=dim), axis, backward)  7.68 us
    dot_general x4, matrix products, row_site(): jnp.einsum('rw,swu->sru', state_rows, site_map, precision=lax.Precision.H...  7.66 us
    ppermute x3, local copies, waits for them, and re-layouts, local(): lax.ppermute(ring[-1], 'site', [(dev, (dev + 1) % 4) for dev in range(4)])  6.44 us
    unnamed x20, local copies, waits for them, and re-layouts  5.3 us
  transfers between devices with their start and end apart: 11, of which 11 were waited for; matrix products, arithmetic and copies ran while one was open for 4% of the time, Pallas kernels for 0%

profile of v1, /device:TPU:8, one launch (start us, length us, event | category | flops | bytes accessed | tf_op | source)
XLA Modules:
  0.0 131.5 jit_solution(14924236979588808242)
XLA Ops:
  0.0 2.9 %fusion.12 = f32[256,8,256]{2,1,0:T(8,128)S(1)} fusion(bf16[1,256,32,256]{3,2,1,0:T(8,128)(2,1)} %param.7, bf16[1,32,8]{1,2,0:T(8,128)(2,1)} %param.8), kind=kOutput, calls=%fused_computation.15 | convolution fusion | flops 33554432 | bytes 6291968 | tf_op jit(solution)/shard_map/jwpv,jpl->jwlv/dot_general | solution.py:22
  3.0 1.7 %fusion.10 = f32[8,256,256]{2,1,0:T(8,128)S(1)} fusion(f32[256,8,256]{2,1,0:T(8,128)S(1)} %fusion.12, bf16[256,8,256]{2,1,0:T(8,128)(2,1)S(1)} %bitcast.46), kind=kOutput, calls=%fused_computation.13 | convolution fusion | flops 1610612736 | bytes 5242880 | tf_op jit(solution)/shard_map/jwlv,jvlu,jls->jswu/dot_general | solution.py:29
  4.7 2.0 %copy.24 = f32[8,256,256]{1,0,2:T(8,128)} copy(f32[8,256,256]{2,1,0:T(8,128)S(1)} %fusion.10) | data formatting | bytes 4194304 | tf_op jit(solution)/shard_map/jwlv,jvlu,jls->jswu/dot_general | solution.py:29
  6.7 2.7 %fusion.15 = f32[1,3,256,256]{2,1,3,0:T(4,128)S(1)} fusion(f32[8,256,256]{1,0,2:T(8,128)} %copy.24, s32[8]{0:T(128)S(1)} %bitcast.47, s32[3]{0:T(128)S(1)} %iota_add_fusion), kind=kOutput, calls=%fused_computation.16 | convolution fusion | flops 18874392 | bytes 2883628 | tf_op jit(solution)/shard_map/jwlv,jvlu,jls->jswu/dot_general | solution.py:29
  9.7 1.5 %collective-permute-start.2 = (f32[1,3,256,256]{3,2,1,0:T(8,128)S(1)}, f32[1,3,256,256]{3,2,1,0:T(8,128)S(1)}, u32[]{:S(2)}, u32[]{:S(2)}) collective-permute-start(f32[1,3,256,256]{3,2,1,0:T(8,128)S(1)} %copy.12), channel_id=1, source_target_pairs={{0,8},{8,16},{16,24},{24,0},{1,9},{9,17},{17,25},{25,1},{2,10},{10... | collective-permute-start | bytes 2359304 | tf_op jit(solution)/shard_map/ppermute | solution.py:34
  11.3 18.7 %collective-permute-done.2 = f32[1,3,256,256]{3,2,1,0:T(8,128)S(1)} collective-permute-done((f32[1,3,256,256]{3,2,1,0:T(8,128)S(1)}, f32[1,3,256,256]{3,2,1,0:T(8,128)S(1)}, u32[]{:S(2)}, u32[]{:S(2)}) %collective-permute-start.2) | collective-permute-done | bytes 786464 | tf_op jit(solution)/shard_map/ppermute | solution.py:34
  31.5 18.8 %collective-permute-done.3 = f32[1,3,256,256]{3,2,1,0:T(8,128)} collective-permute-done((f32[1,3,256,256]{3,2,1,0:T(8,128)S(1)}, f32[1,3,256,256]{3,2,1,0:T(8,128)}, u32[]{:S(2)}, u32[]{:S(2)}) %collective-permute-start.3) | collective-permute-done | bytes 786464 | tf_op jit(solution)/shard_map/ppermute | solution.py:34
  51.3 1.5 %copy.15 = f32[1,3,256,256]{2,1,3,0:T(4,128)S(1)} copy(f32[1,3,256,256]{3,2,1,0:T(8,128)} %copy-done.3) | data formatting | bytes 1572864 | tf_op jit(solution)/shard_map/ppermute | solution.py:34
  52.8 2.4 %copy.14 = f32[1,3,256,256]{2,1,3,0:T(4,128)} copy(f32[1,3,256,256]{3,2,1,0:T(8,128)} %collective-permute-done.3) | data formatting | bytes 1572864 | tf_op jit(solution)/shard_map/ppermute | solution.py:34
  55.3 13.8 %collective-permute-done.4 = f32[1,3,256,256]{3,2,1,0:T(8,128)} collective-permute-done((f32[1,3,256,256]{3,2,1,0:T(8,128)}, f32[1,3,256,256]{3,2,1,0:T(8,128)}, u32[]{:S(2)}, u32[]{:S(2)}) %collective-permute-start.4) | collective-permute-done | bytes 786464 | tf_op jit(solution)/shard_map/ppermute | solution.py:34
  69.1 2.5 %copy.13 = f32[1,3,256,256]{2,1,3,0:T(4,128)} copy(f32[1,3,256,256]{3,2,1,0:T(8,128)} %collective-permute-done.4) | data formatting | bytes 1572864 | tf_op jit(solution)/shard_map/ppermute | solution.py:34
  71.5 1.6 %constant_dynamic-update-slice_fusion.8 = f32[8,3,256,256]{2,1,3,0:T(4,128)S(1)} fusion(f32[1,3,256,256]{2,1,3,0:T(4,128)} %copy.13), kind=kLoop, calls=%fused_computation.25 | loop fusion | bytes 1835008
  73.1 1.5 %constant_dynamic-update-slice_fusion.7 = f32[8,3,256,256]{2,1,3,0:T(4,128)S(1)} fusion(f32[8,3,256,256]{2,1,3,0:T(4,128)S(1)} %constant_dynamic-update-slice_fusion.8, f32[1,3,256,256]{2,1,3,0:T(4,128)} %copy.14), kind=kLoop, calls=%fused_computation.24 | loop fusion | bytes 1835008
  76.9 2.2 %copy.19 = f32[4,3,256,256]{2,3,1,0:T(8,128)} copy(f32[4,3,256,256]{2,1,3,0:T(4,128)S(1)} %constant_dynamic-slice_fusion) | data formatting | bytes 6291456 | tf_op jit(solution)/shard_map/while | solution.py:50
  79.1 40.8 %while.12 = (s32[]{:T(128)}, f32[128,256]{0,1:T(8,128)S(1)}, f32[4,128,256]{1,2,0:T(8,128)S(1)}, f32[4,3,256,256]{2,3,1,0:T(8,128)}, s32[]{:T(128)}) while((s32[]{:T(128)}, f32[128,256]{0,1:T(8,128)S(1)}, f32[4,128,256]{1,2,0:T(8,128)S(1)}, f32[4,3,256,256]{2,3,1,0:T(8,128)}, s32[]{:T(128)}) %tuple.29), condition=%wide.region_1.2_spmd, body=%wide.region_0.1_spmd.sunk | while | flops 302055424 | bytes 3539101 | solution.py:50
  79.1 1.9 %convolution_bitcast_fusion.2 = f32[3,128,256]{1,2,0:T(8,128)S(1)} fusion(f32[4,3,256,256]{2,3,1,0:T(8,128)} %get-tuple-element.94, s32[]{:T(128)S(6)} %copy.42, f32[128,256]{0,1:T(8,128)S(1)} %get-tuple-element.87), kind=kOutput, calls=%fused_computation.clone.1 | convolution fusion | flops 301989888 | bytes 1310724 | tf_op jit(solution)/shard_map/while/body/eval_jaxpr/rw,swu->sru/dot_general | solution.py:44
  81.0 1.9 %collective-permute-start = (f32[1,128,256]{1,2,0:T(8,128)S(1)}, f32[1,128,256]{1,2,0:T(8,128)S(1)}, u32[]{:S(2)}, u32[]{:S(2)}) collective-permute-start(f32[1,128,256]{1,2,0:T(8,128)S(1)} %get-tuple-element.77), channel_id=1, source_target_pairs={{1,0},{2,1},{3,2},{4,3},{5,4},{6,5},{7,6},{9,8},{10,9},{11,10},{12... | collective-permute-start | bytes 393224 | tf_op jit(solution)/shard_map/while/body/eval_jaxpr/ppermute | solution.py:15
  83.0 2.4 %collective-permute-start.1 = (f32[1,128,256]{1,2,0:T(8,128)S(1)}, f32[1,128,256]{1,2,0:T(8,128)S(1)}, u32[]{:S(2)}, u32[]{:S(2)}) collective-permute-start(f32[1,128,256]{1,2,0:T(8,128)S(1)} %get-tuple-element.78), channel_id=1, source_target_pairs={{0,1},{1,2},{2,3},{3,4},{4,5},{5,6},{6,7},{8,9},{9,10},{10,11},{11... | collective-permute-start | bytes 393224 | tf_op jit(solution)/shard_map/while/body/eval_jaxpr/ppermute | solution.py:12
  85.5 3.8 %collective-permute-done.1 = f32[1,128,256]{1,2,0:T(8,128)S(1)} collective-permute-done((f32[1,128,256]{1,2,0:T(8,128)S(1)}, f32[1,128,256]{1,2,0:T(8,128)S(1)}, u32[]{:S(2)}, u32[]{:S(2)}) %collective-permute-start.1) | collective-permute-done | bytes 131104 | tf_op jit(solution)/shard_map/while/body/eval_jaxpr/ppermute | solution.py:12
  89.3 1.9 %convolution_bitcast_fusion.2 = f32[3,128,256]{1,2,0:T(8,128)S(1)} fusion(f32[4,3,256,256]{2,3,1,0:T(8,128)} %get-tuple-element.94, s32[]{:T(128)S(6)} %copy.42, f32[128,256]{0,1:T(8,128)S(1)} %get-tuple-element.87), kind=kOutput, calls=%fused_computation.clone.1 | convolution fusion | flops 301989888 | bytes 1310724 | tf_op jit(solution)/shard_map/while/body/eval_jaxpr/rw,swu->sru/dot_general | solution.py:44
  91.2 1.9 %collective-permute-start = (f32[1,128,256]{1,2,0:T(8,128)S(1)}, f32[1,128,256]{1,2,0:T(8,128)S(1)}, u32[]{:S(2)}, u32[]{:S(2)}) collective-permute-start(f32[1,128,256]{1,2,0:T(8,128)S(1)} %get-tuple-element.77), channel_id=1, source_target_pairs={{1,0},{2,1},{3,2},{4,3},{5,4},{6,5},{7,6},{9,8},{10,9},{11,10},{12... | collective-permute-start | bytes 393224 | tf_op jit(solution)/shard_map/while/body/eval_jaxpr/ppermute | solution.py:15
  93.2 2.4 %collective-permute-start.1 = (f32[1,128,256]{1,2,0:T(8,128)S(1)}, f32[1,128,256]{1,2,0:T(8,128)S(1)}, u32[]{:S(2)}, u32[]{:S(2)}) collective-permute-start(f32[1,128,256]{1,2,0:T(8,128)S(1)} %get-tuple-element.78), channel_id=1, source_target_pairs={{0,1},{1,2},{2,3},{3,4},{4,5},{5,6},{6,7},{8,9},{9,10},{10,11},{11... | collective-permute-start | bytes 393224 | tf_op jit(solution)/shard_map/while/body/eval_jaxpr/ppermute | solution.py:12
  95.7 3.8 %collective-permute-done.1 = f32[1,128,256]{1,2,0:T(8,128)S(1)} collective-permute-done((f32[1,128,256]{1,2,0:T(8,128)S(1)}, f32[1,128,256]{1,2,0:T(8,128)S(1)}, u32[]{:S(2)}, u32[]{:S(2)}) %collective-permute-start.1) | collective-permute-done | bytes 131104 | tf_op jit(solution)/shard_map/while/body/eval_jaxpr/ppermute | solution.py:12
  99.5 1.9 %convolution_bitcast_fusion.2 = f32[3,128,256]{1,2,0:T(8,128)S(1)} fusion(f32[4,3,256,256]{2,3,1,0:T(8,128)} %get-tuple-element.94, s32[]{:T(128)S(6)} %copy.42, f32[128,256]{0,1:T(8,128)S(1)} %get-tuple-element.87), kind=kOutput, calls=%fused_computation.clone.1 | convolution fusion | flops 301989888 | bytes 1310724 | tf_op jit(solution)/shard_map/while/body/eval_jaxpr/rw,swu->sru/dot_general | solution.py:44
  101.4 1.9 %collective-permute-start = (f32[1,128,256]{1,2,0:T(8,128)S(1)}, f32[1,128,256]{1,2,0:T(8,128)S(1)}, u32[]{:S(2)}, u32[]{:S(2)}) collective-permute-start(f32[1,128,256]{1,2,0:T(8,128)S(1)} %get-tuple-element.77), channel_id=1, source_target_pairs={{1,0},{2,1},{3,2},{4,3},{5,4},{6,5},{7,6},{9,8},{10,9},{11,10},{12... | collective-permute-start | bytes 393224 | tf_op jit(solution)/shard_map/while/body/eval_jaxpr/ppermute | solution.py:15
  103.4 2.4 %collective-permute-start.1 = (f32[1,128,256]{1,2,0:T(8,128)S(1)}, f32[1,128,256]{1,2,0:T(8,128)S(1)}, u32[]{:S(2)}, u32[]{:S(2)}) collective-permute-start(f32[1,128,256]{1,2,0:T(8,128)S(1)} %get-tuple-element.78), channel_id=1, source_target_pairs={{0,1},{1,2},{2,3},{3,4},{4,5},{5,6},{6,7},{8,9},{9,10},{10,11},{11... | collective-permute-start | bytes 393224 | tf_op jit(solution)/shard_map/while/body/eval_jaxpr/ppermute | solution.py:12
  105.9 3.8 %collective-permute-done.1 = f32[1,128,256]{1,2,0:T(8,128)S(1)} collective-permute-done((f32[1,128,256]{1,2,0:T(8,128)S(1)}, f32[1,128,256]{1,2,0:T(8,128)S(1)}, u32[]{:S(2)}, u32[]{:S(2)}) %collective-permute-start.1) | collective-permute-done | bytes 131104 | tf_op jit(solution)/shard_map/while/body/eval_jaxpr/ppermute | solution.py:12
  109.7 1.9 %convolution_bitcast_fusion.2 = f32[3,128,256]{1,2,0:T(8,128)S(1)} fusion(f32[4,3,256,256]{2,3,1,0:T(8,128)} %get-tuple-element.94, s32[]{:T(128)S(6)} %copy.42, f32[128,256]{0,1:T(8,128)S(1)} %get-tuple-element.87), kind=kOutput, calls=%fused_computation.clone.1 | convolution fusion | flops 301989888 | bytes 1310724 | tf_op jit(solution)/shard_map/while/body/eval_jaxpr/rw,swu->sru/dot_general | solution.py:44
  111.7 1.9 %collective-permute-start = (f32[1,128,256]{1,2,0:T(8,128)S(1)}, f32[1,128,256]{1,2,0:T(8,128)S(1)}, u32[]{:S(2)}, u32[]{:S(2)}) collective-permute-start(f32[1,128,256]{1,2,0:T(8,128)S(1)} %get-tuple-element.77), channel_id=1, source_target_pairs={{1,0},{2,1},{3,2},{4,3},{5,4},{6,5},{7,6},{9,8},{10,9},{11,10},{12... | collective-permute-start | bytes 393224 | tf_op jit(solution)/shard_map/while/body/eval_jaxpr/ppermute | solution.py:15
  113.6 2.4 %collective-permute-start.1 = (f32[1,128,256]{1,2,0:T(8,128)S(1)}, f32[1,128,256]{1,2,0:T(8,128)S(1)}, u32[]{:S(2)}, u32[]{:S(2)}) collective-permute-start(f32[1,128,256]{1,2,0:T(8,128)S(1)} %get-tuple-element.78), channel_id=1, source_target_pairs={{0,1},{1,2},{2,3},{3,4},{4,5},{5,6},{6,7},{8,9},{9,10},{10,11},{11... | collective-permute-start | bytes 393224 | tf_op jit(solution)/shard_map/while/body/eval_jaxpr/ppermute | solution.py:12
  116.1 3.8 %collective-permute-done.1 = f32[1,128,256]{1,2,0:T(8,128)S(1)} collective-permute-done((f32[1,128,256]{1,2,0:T(8,128)S(1)}, f32[1,128,256]{1,2,0:T(8,128)S(1)}, u32[]{:S(2)}, u32[]{:S(2)}) %collective-permute-start.1) | collective-permute-done | bytes 131104 | tf_op jit(solution)/shard_map/while/body/eval_jaxpr/ppermute | solution.py:12
  119.9 10.6 %all_to_all.12 = f32[4,128,256]{1,2,0:T(8,128)S(1)} all-to-all(f32[4,128,256]{1,2,0:T(8,128)S(1)} %get-tuple-element.27), channel_id=1, replica_groups=mesh['site'=4,'sector'=8] {'site'}, dimensions={0} | all-to-all | bytes 1048576 | tf_op jit(solution)/shard_map/all_to_all | solution.py:51
  (40 shorter events, 6.5 us)
Async XLA Ops:
  0.0 3.0 %copy-start = (bf16[1,256,8,256]{3,2,1,0:T(8,128)(2,1)S(1)}, bf16[1,256,8,256]{3,2,1,0:T(8,128)(2,1)}, u32[]{:S(2)}) copy-start(bf16[1,256,8,256]{3,2,1,0:T(8,128)(2,1)} %param.9) | copy-start | bytes 3145732
  0.0 6.7 %copy-start.5 = (s32[1,8]{1,0:T(1,128)S(1)}, s32[1,8]{1,0:T(1,128)}, u32[]{:S(2)}) copy-start(s32[1,8]{1,0:T(1,128)} %param.10) | copy-start | bytes 100
  9.7 20.2 %collective-permute-start.2 = (f32[1,3,256,256]{3,2,1,0:T(8,128)S(1)}, f32[1,3,256,256]{3,2,1,0:T(8,128)S(1)}, u32[]{:S(2)}, u32[]{:S(2)}) collective-permute-start(f32[1,3,256,256]{3,2,1,0:T(8,128)S(1)} %copy.12), channel_id=1, source_target_pairs={{0,8},{8,16},{16,24},{24,0},{1,9},{9,17},{17,25},{25,1},{2,10},{10... | collective-permute-start | bytes 2359304 | tf_op jit(solution)/shard_map/ppermute | solution.py:34
  30.0 0.9 copy-start.3
  30.9 19.4 %collective-permute-start.3 = (f32[1,3,256,256]{3,2,1,0:T(8,128)S(1)}, f32[1,3,256,256]{3,2,1,0:T(8,128)}, u32[]{:S(2)}, u32[]{:S(2)}) collective-permute-start(f32[1,3,256,256]{3,2,1,0:T(8,128)S(1)} %collective-permute-done.2), channel_id=1, source_target_pairs={{0,8},{8,16},{16,24},{24,0},{1,9},{9,17},{17,25},{25,1},{2,10},{10... | collective-permute-start | bytes 2359304 | tf_op jit(solution)/shard_map/ppermute | solution.py:34
  50.3 18.8 %collective-permute-start.4 = (f32[1,3,256,256]{3,2,1,0:T(8,128)}, f32[1,3,256,256]{3,2,1,0:T(8,128)}, u32[]{:S(2)}, u32[]{:S(2)}) collective-permute-start(f32[1,3,256,256]{3,2,1,0:T(8,128)} %collective-permute-done.3), channel_id=1, source_target_pairs={{0,8},{8,16},{16,24},{24,0},{1,9},{9,17},{17,25},{25,1},{2,10},{10... | collective-permute-start | bytes 2359304 | tf_op jit(solution)/shard_map/ppermute | solution.py:34
  71.5 3.6 %copy-start.2 = (f32[1,3,256,256]{2,1,3,0:T(4,128)S(1)}, f32[1,3,256,256]{2,1,3,0:T(4,128)}, u32[]{:S(2)}) copy-start(f32[1,3,256,256]{2,1,3,0:T(4,128)} %copy.13) | copy-start | bytes 2359300
  71.5 3.8 %copy-start.1 = (f32[1,3,256,256]{2,1,3,0:T(4,128)S(1)}, f32[1,3,256,256]{2,1,3,0:T(4,128)}, u32[]{:S(2)}) copy-start(f32[1,3,256,256]{2,1,3,0:T(4,128)} %copy.14) | copy-start | bytes 2359300
  76.1 2.9 %copy-start.4 = (f32[4,128,256]{1,2,0:T(8,128)S(1)}, f32[4,128,256]{1,2,0:T(8,128)}, u32[]{:S(2)}) copy-start(f32[4,128,256]{1,2,0:T(8,128)} %custom-call.1) | copy-start | bytes 1572868
  81.0 4.4 %collective-permute-start = (f32[1,128,256]{1,2,0:T(8,128)S(1)}, f32[1,128,256]{1,2,0:T(8,128)S(1)}, u32[]{:S(2)}, u32[]{:S(2)}) collective-permute-start(f32[1,128,256]{1,2,0:T(8,128)S(1)} %get-tuple-element.77), channel_id=1, source_target_pairs={{1,0},{2,1},{3,2},{4,3},{5,4},{6,5},{7,6},{9,8},{10,9},{11,10},{12... | collective-permute-start | bytes 393224 | tf_op jit(solution)/shard_map/while/body/eval_jaxpr/ppermute | solution.py:15
  83.0 6.3 %collective-permute-start.1 = (f32[1,128,256]{1,2,0:T(8,128)S(1)}, f32[1,128,256]{1,2,0:T(8,128)S(1)}, u32[]{:S(2)}, u32[]{:S(2)}) collective-permute-start(f32[1,128,256]{1,2,0:T(8,128)S(1)} %get-tuple-element.78), channel_id=1, source_target_pairs={{0,1},{1,2},{2,3},{3,4},{4,5},{5,6},{6,7},{8,9},{9,10},{10,11},{11... | collective-permute-start | bytes 393224 | tf_op jit(solution)/shard_map/while/body/eval_jaxpr/ppermute | solution.py:12
  91.2 4.4 %collective-permute-start = (f32[1,128,256]{1,2,0:T(8,128)S(1)}, f32[1,128,256]{1,2,0:T(8,128)S(1)}, u32[]{:S(2)}, u32[]{:S(2)}) collective-permute-start(f32[1,128,256]{1,2,0:T(8,128)S(1)} %get-tuple-element.77), channel_id=1, source_target_pairs={{1,0},{2,1},{3,2},{4,3},{5,4},{6,5},{7,6},{9,8},{10,9},{11,10},{12... | collective-permute-start | bytes 393224 | tf_op jit(solution)/shard_map/while/body/eval_jaxpr/ppermute | solution.py:15
  93.2 6.3 %collective-permute-start.1 = (f32[1,128,256]{1,2,0:T(8,128)S(1)}, f32[1,128,256]{1,2,0:T(8,128)S(1)}, u32[]{:S(2)}, u32[]{:S(2)}) collective-permute-start(f32[1,128,256]{1,2,0:T(8,128)S(1)} %get-tuple-element.78), channel_id=1, source_target_pairs={{0,1},{1,2},{2,3},{3,4},{4,5},{5,6},{6,7},{8,9},{9,10},{10,11},{11... | collective-permute-start | bytes 393224 | tf_op jit(solution)/shard_map/while/body/eval_jaxpr/ppermute | solution.py:12
  101.4 4.4 %collective-permute-start = (f32[1,128,256]{1,2,0:T(8,128)S(1)}, f32[1,128,256]{1,2,0:T(8,128)S(1)}, u32[]{:S(2)}, u32[]{:S(2)}) collective-permute-start(f32[1,128,256]{1,2,0:T(8,128)S(1)} %get-tuple-element.77), channel_id=1, source_target_pairs={{1,0},{2,1},{3,2},{4,3},{5,4},{6,5},{7,6},{9,8},{10,9},{11,10},{12... | collective-permute-start | bytes 393224 | tf_op jit(solution)/shard_map/while/body/eval_jaxpr/ppermute | solution.py:15
  103.4 6.3 %collective-permute-start.1 = (f32[1,128,256]{1,2,0:T(8,128)S(1)}, f32[1,128,256]{1,2,0:T(8,128)S(1)}, u32[]{:S(2)}, u32[]{:S(2)}) collective-permute-start(f32[1,128,256]{1,2,0:T(8,128)S(1)} %get-tuple-element.78), channel_id=1, source_target_pairs={{0,1},{1,2},{2,3},{3,4},{4,5},{5,6},{6,7},{8,9},{9,10},{10,11},{11... | collective-permute-start | bytes 393224 | tf_op jit(solution)/shard_map/while/body/eval_jaxpr/ppermute | solution.py:12
  111.7 4.4 %collective-permute-start = (f32[1,128,256]{1,2,0:T(8,128)S(1)}, f32[1,128,256]{1,2,0:T(8,128)S(1)}, u32[]{:S(2)}, u32[]{:S(2)}) collective-permute-start(f32[1,128,256]{1,2,0:T(8,128)S(1)} %get-tuple-element.77), channel_id=1, source_target_pairs={{1,0},{2,1},{3,2},{4,3},{5,4},{6,5},{7,6},{9,8},{10,9},{11,10},{12... | collective-permute-start | bytes 393224 | tf_op jit(solution)/shard_map/while/body/eval_jaxpr/ppermute | solution.py:15
  113.6 6.3 %collective-permute-start.1 = (f32[1,128,256]{1,2,0:T(8,128)S(1)}, f32[1,128,256]{1,2,0:T(8,128)S(1)}, u32[]{:S(2)}, u32[]{:S(2)}) collective-permute-start(f32[1,128,256]{1,2,0:T(8,128)S(1)} %get-tuple-element.78), channel_id=1, source_target_pairs={{0,1},{1,2},{2,3},{3,4},{4,5},{5,6},{6,7},{8,9},{9,10},{10,11},{11... | collective-permute-start | bytes 393224 | tf_op jit(solution)/shard_map/while/body/eval_jaxpr/ppermute | solution.py:12
